TPU v7x, 512 devices: a whole 4x4x16 slice. The times are simulated.
512 devices in a mesh: row: 32 (over x, z_hi, core), col: 16 (over z_lo, y).
Axes of the slice: x: 4, y: 4, z: 16 (z_hi: 4, z_lo: 4; z = z_hi * 4 + z_lo), core: 2. Of those that a mesh axis runs over, the one named last changes fastest.
Arguments:
- top_inverse: float32 [2, 4096, 4096], P(None, 'row', 'col'), may hold values from -6 to 6
- panel: float32 [2, 2048, 8192], P(None, 'row', 'col'), may hold values from -0.09375 to 0.09375
- leaf_rows: int32 [32, 8], P('col'), may hold values from 0 to 15, as said below
- leaf_counts: int32 [32], P('col'), may hold values from 1 to 8, as said below
- diag_inverse: float32 [2, 256, 8192], P(None, 'row', 'col'), may hold values from -6 to 6
Outputs:
- selected: float32 [2, 4096, 8192], P(None, 'row', 'col')
- diagonal: float32 [2, 256, 8192], P(None, 'row', 'col')
Inputs may be any that keep to these rules, and one draw needn't show every extreme that they name: `leaf_rows`: the 8 entries of each leaf are distinct separator blocks. Slots 0 to leaf_counts - 1 of a leaf are live.
All inputs are finite; a program needn't handle non-finite values.
Results may differ from a plain program's by a relative error of at most 0.0003.
Values sent between devices are 32-bit elements; how exact they have to be, the bound alone decides.
A program may use at most 128 MiB of HBM per device.

v0:
```python
import jax
import jax.numpy as jnp
from jax import lax
from jax.sharding import PartitionSpec as P

B = 256
ROW_DEV = 128
LEAF_COL = 2


def product_highest(left, right):
    return jnp.dot(left, right, precision=lax.Precision.HIGHEST, preferred_element_type=jnp.float32)


def complex_product(left_real, left_imag, right_real, right_imag):
    real_part = product_highest(left_real, right_real) - product_highest(left_imag, right_imag)
    imag_part = product_highest(left_real, right_imag) + product_highest(left_imag, right_real)
    return (real_part, imag_part)


def on_device(top_inverse, panel, leaf_rows, leaf_counts, diag_inverse):
    slot_count = leaf_rows.shape[1]
    row_index = lax.axis_index("row")
    first_row = row_index * ROW_DEV
    my_block = first_row // B
    offset = first_row % B
    active_slots = jnp.arange(slot_count, dtype=jnp.int32)[None, :] < leaf_counts[:, None]
    block_live = jnp.any((leaf_rows == my_block) & active_slots, axis=1)
    targets = jnp.arange(ROW_DEV, dtype=jnp.int32)
    top_strip = lax.all_gather(top_inverse, "col", axis=2, tiled=True)
    section = lax.all_gather(panel, "row", axis=1, tiled=True)
    length = section.shape[1]
    gains_prod = []
    gains_low = []
    for absorb_member in range(LEAF_COL):
        position = jnp.arange(length, dtype=jnp.int32)
        slot_index = position // B
        slot_within = position % B
        slot_target_block = jnp.take(leaf_rows[absorb_member], slot_index)
        slot_active = slot_index < leaf_counts[absorb_member]
        columns = slot_target_block * B + slot_within
        panel_part = (
            section[:, :, absorb_member * B : (absorb_member + 1) * B]
            * slot_active.astype(jnp.float32)[None, :, None]
        )
        picked = jnp.take(top_strip, columns, axis=2)
        real_part, imag_part = complex_product(picked[0], picked[1], panel_part[0], panel_part[1])
        gain_prod = jnp.stack([real_part, imag_part])
        owned = slot_active & (slot_target_block == my_block)
        select = ((slot_within[None, :] - offset == targets[:, None]) & owned[None, :]).astype(
            jnp.float32
        )
        gain_low = jnp.stack(
            [product_highest(select, panel_part[0]), product_highest(select, panel_part[1])]
        )
        gains_prod.append(gain_prod)
        gains_low.append(gain_low)
    product = jnp.concatenate(gains_prod, axis=2)
    lower_rows = jnp.concatenate(gains_low, axis=2)
    keep_rows = jnp.repeat(block_live.astype(jnp.float32), B)
    selected = -product * keep_rows[None, None, :]
    diag_parts = []
    for member in range(LEAF_COL):
        sel_block = selected[:, :, member * B : (member + 1) * B]
        low_block = lower_rows[:, :, member * B : (member + 1) * B]
        diag_real, diag_imag = complex_product(
            sel_block[0].T, sel_block[1].T, low_block[0], low_block[1]
        )
        diag_parts.append(jnp.stack([diag_real, diag_imag]))
    partial_diag = jnp.concatenate(diag_parts, axis=2)
    total_sum = lax.psum(partial_diag, "row")
    share_rows = diag_inverse.shape[1]
    share_sum = lax.dynamic_slice_in_dim(total_sum, row_index * share_rows, share_rows, 1)
    return (selected, diag_inverse - share_sum)


def solution(mesh):
    return jax.shard_map(
        on_device,
        mesh=mesh,
        in_specs=(
            P(None, "row", "col"),
            P(None, "row", "col"),
            P("col", None),
            P("col"),
            P(None, "row", "col"),
        ),
        out_specs=(P(None, "row", "col"), P(None, "row", "col")),
        check_vma=False,
    )
```

profile of v0, /device:TPU:1, one launch (start us, length us, event | category | flops | bytes accessed | tf_op | source)
XLA Modules:
  0.0 626.7 jit_solution(4336711945029545441)
XLA Ops:
  7.2 0.0 all-gather.3.cloned.1.call-start
  7.2 1.8 copy.12
  9.0 0.0 all-gather.3.cloned.1.call-update
  9.0 0.0 all-gather.5.cloned.1.call-start
  9.1 0.7 all-gather.5.cloned.1.call-update
  9.8 0.0 all-reduce.2.cloned.1.call-start
  9.8 0.9 and_reduce_fusion
  10.7 0.1 broadcast_bitcast_fusion
  10.8 0.8 slice_bitcast_fusion.45
  11.6 0.7 fusion.70
  12.3 5.2 compare_and_fusion.1
  17.4 1.4 fusion.69
  18.8 5.7 compare_and_fusion.3
  24.5 4.9 compare_and_fusion
  29.4 5.5 compare_and_fusion.2
  35.0 4.9 broadcast_clamp_fusion
  39.9 5.2 broadcast_clamp_fusion.1
  45.1 1.2 fusion.65
  46.3 52.9 %all-gather.3.cloned.1.call-done = f32[2,128,4096]{1,0,2:T(2,128)} async-done(((f32[2,128,256]{1,0,2:T(2,128)}), f32[2,128,4096]{1,0,2:T(2,128)}) %all-gather.3.cloned.1.call-update) | async-done | bytes 4194320 | tf_op jit(solution)/shard_map/all_gather | solution.py:30
  99.2 9.0 %gather_fusion.1 = f32[2048,2,128]{2,1,0:T(2,128)S(1)} fusion(f32[2,128,4096]{1,0,2:T(2,128)} %all-gather.3.cloned.1.call-done, s32[2048]{0:T(1024)S(1)} %broadcast_clamp_fusion), kind=kCustom, calls=%fused_computation.1.clone | custom fusion | bytes 4202496 | tf_op jit(solution)/shard_map/jit(_take)/gather | solution.py:46
  108.2 16.7 %gather_fusion = f32[2048,2,128]{2,1,0:T(2,128)} fusion(f32[2,128,4096]{1,0,2:T(2,128)} %all-gather.3.cloned.1.call-done, s32[2048]{0:T(1024)S(1)} %broadcast_clamp_fusion.1), kind=kCustom, calls=%fused_computation.clone | custom fusion | bytes 4202496 | tf_op jit(solution)/shard_map/jit(_take)/gather | solution.py:46
  124.9 7.4 %select_bitcast_fusion = f32[2,128,2048]{1,0,2:T(2,128)S(1)} fusion(f32[2048,2,128]{2,1,0:T(2,128)S(1)} %gather_fusion.1, pred[2048]{0:T(1024)(128)(4,1)S(1)} %compare_and_fusion), kind=kLoop, calls=%fused_computation.8 | loop fusion | flops 524288 | bytes 4196352 | tf_op jit(solution)/shard_map/jit(_take)/select_n | solution.py:46
  132.3 0.0 copy-start.1
  132.3 1.7 fusion.68
  134.0 0.0 copy-done.1
  134.0 7.4 %select_bitcast_fusion.1 = f32[2,128,2048]{1,0,2:T(2,128)S(1)} fusion(f32[2048,2,128]{2,1,0:T(2,128)S(1)} %copy-done.1, pred[2048]{0:T(1024)(128)(4,1)S(1)} %compare_and_fusion.1), kind=kLoop, calls=%fused_computation.9 | loop fusion | flops 524288 | bytes 4196352 | tf_op jit(solution)/shard_map/jit(_take)/select_n | solution.py:46
  141.5 2.5 fusion.67
  144.0 102.6 %all-gather.5.cloned.1.call-done = f32[2,2048,512]{2,1,0:T(8,128)} async-done(((f32[2,64,512]{2,1,0:T(8,128)}), f32[2,2048,512]{2,1,0:T(8,128)}) %all-gather.5.cloned.1.call-update) | async-done | bytes 8388624 | tf_op jit(solution)/shard_map/all_gather | solution.py:31
  246.6 4.1 slice_multiply_fusion.1
  250.7 1.0 fusion.3
  251.7 1.0 fusion
  252.7 1.0 fusion.9
  253.7 1.0 fusion.6
  254.8 0.0 copy-start
  254.8 1.9 fusion.1
  256.6 0.0 copy-done
  256.6 1.9 fusion.2
  258.6 1.9 fusion.23
  260.5 1.9 fusion.21
  262.4 2.1 fusion.7
  264.5 1.9 fusion.8
  266.3 1.9 fusion.19
  268.2 1.9 fusion.17
  270.1 0.1 fusion.30
  270.1 0.0 copy-start.2
  270.1 0.4 fusion.41
  270.6 0.4 fusion.42
  271.0 0.4 fusion.12
  271.4 0.4 fusion.13
  271.8 0.4 fusion.39
  272.3 0.4 fusion.40
  272.7 0.4 fusion.14
  273.1 0.0 copy-done.2
  273.1 0.0 copy-start.3
  273.1 0.4 fusion.15
  273.5 1.1 maximum_maximum_fusion
  274.6 0.0 all-reduce.2.cloned.1.call-update
  274.6 0.0 copy-done.3
  274.7 0.2 copy.13
  274.9 343.3 %all-reduce.2.cloned.1.call-done = f32[2,256,512]{1,2,0:T(8,128)} async-done(((f32[2,256,512]{1,2,0:T(8,128)}), f32[2,256,512]{1,2,0:T(8,128)}) %all-reduce.2.cloned.1.call-update) | async-done | bytes 1048592 | tf_op jit(solution)/shard_map/psum | solution.py:71
  618.2 1.2 dynamic-slice_subtract_fusion
  619.4 0.8 copy.14
  (3 shorter events, 0.0 us)
Async XLA Ops:
  7.2 92.1 %all-gather.3.cloned.1.call-start = ((), (), s32[]{:S(2)}) async-start(), calls=%async_computation | async-start | bytes 4456448 | tf_op jit(solution)/shard_map/all_gather | solution.py:30
  9.0 237.5 %all-gather.5.cloned.1.call-start = ((), (), s32[]{:S(2)}) async-start(), calls=%async_computation.1 | async-start | bytes 8650752 | tf_op jit(solution)/shard_map/all_gather | solution.py:31
  9.8 608.4 %all-reduce.2.cloned.1.call-start = ((), (), s32[]{:S(2)}) async-start(), calls=%async_computation.2 | async-start | bytes 2097152 | tf_op jit(solution)/shard_map/psum | solution.py:71
  132.3 1.7 copy-start.1
  254.8 1.9 copy-start
  270.1 3.0 copy-start.2
  273.1 1.5 copy-start.3
Sparse Core Ops, SparseCore 0:
  10.6 88.5 all-gather.2
  102.5 144.0 all-gather.4
  274.8 343.3 all-reduce.1
where the time goes:
time: 627 us
  waiting for transfers between devices  500 us (80%)
  other arithmetic  54.8 us (9%)
  local copies, waits for them, and re-layouts  35.5 us (6%)
  matrix products  22.6 us (4%)
  between operations  14.1 us (2%)
    psum x1, waiting for transfers between devices, on_device(): total_sum = lax.psum(partial_diag, 'row')  343 us
    all_gather x1, waiting for transfers between devices, on_device(): section = lax.all_gather(panel, 'row', axis=1, tiled=True)  103 us
    all_gather x1, waiting for transfers between devices, on_device(): top_strip = lax.all_gather(top_inverse, 'col', axis=2, tiled=True)  52.9 us
    gather x2, local copies, waits for them, and re-layouts, on_device(): picked = jnp.take(top_strip, columns, axis=2)  25.6 us
    dot_general x20, matrix products, product_highest(): jnp.dot(left, right, precision=lax.Precision.HIGHEST, preferred_element_t...  22.6 us
    select_n x2, other arithmetic, on_device(): picked = jnp.take(top_strip, columns, axis=2)  14.9 us
  transfers between devices with their start and end apart: 3, of which 3 were waited for; matrix products, arithmetic and copies ran while one was open for 13% of the time, Pallas kernels for 0%

commit v1 on v0

v1 whole, which is shorter than its diff:
```python
import jax
import jax.numpy as jnp
from jax import lax
from jax.experimental import pallas as pl
from jax.experimental.pallas import tpu as pltpu
from jax.sharding import PartitionSpec as P

MESH = pl.DeviceIdType.MESH
B = 256
SLOTS = 8
LEAVES = 2
RING = 4


def split(value):
    high = value.astype(jnp.bfloat16)
    low = (value - high.astype(jnp.float32)).astype(jnp.bfloat16)
    return high, low


def dot(left, right):
    return jnp.dot(left, right, preferred_element_type=jnp.float32)


def dot_t(left, right):
    return lax.dot_general(
        left, right, (((0,), (0,)), ((), ())), preferred_element_type=jnp.float32
    )


def kernel(
    rows_ref,
    counts_ref,
    top_ref,
    panel_ref,
    diag_ref,
    sel_ref,
    out_ref,
    a_buf,
    l_buf0,
    l_buf1,
    acc,
    d_buf,
    sib_buf,
    c_buf,
    x1_buf,
    x2_buf,
    e_buf,
    z1_buf,
    z2_buf,
    local_sem,
    az_own,
    az_fwd,
    az_recv,
    ay_send,
    ay_recv,
    lz_send,
    lz_recv,
    lx_send,
    lx_recv,
    lc_send,
    lc_recv,
    rs_send,
    rs_recv,
):
    l_buf = (l_buf0, l_buf1)
    row = lax.axis_index("row")
    col = lax.axis_index("col")
    x, zh, c = row // 8, (row // 2) % 4, row % 2
    zl, y = col // 4, col % 4

    def mod4(v):
        return (v + 8) % 4

    def row_of(xx, zz, cc):
        return (mod4(xx) * 4 + mod4(zz)) * 2 + cc

    sib = (row_of(x, zh, 1 - c), col)
    x_dev = {d: (row_of(x + d, zh, c), col) for d in (-1, 1)}
    zh_dev = {d: (row_of(x, zh + d, c), col) for d in (-1, 1)}
    y_dev = {d: (row, zl * 4 + mod4(y + d)) for d in (-1, 1)}

    own = [
        pltpu.make_async_copy(top_ref, a_buf.at[col], local_sem.at[0]),
    ] + [
        pltpu.make_async_copy(
            panel_ref.at[:, :, pl.ds(m * B, B)], l_buf[m].at[row], local_sem.at[1 + m]
        )
        for m in range(LEAVES)
    ]
    for copy in own:
        copy.start()

    barrier = pltpu.get_barrier_semaphore()
    greet = [sib, x_dev[-1], x_dev[1], zh_dev[-1], zh_dev[1], y_dev[-1], y_dev[1]]
    greet += [(row, mod4(zl + d) * 4 + y) for d in (-1, 1)]
    for dev in greet:
        pl.semaphore_signal(barrier, inc=1, device_id=dev, device_id_type=MESH)
    pl.semaphore_wait(barrier, len(greet))
    for copy in own:
        copy.wait()

    sent = []

    def desc(src, dst, ss, rs, dev):
        return pltpu.make_async_remote_copy(
            src_ref=src,
            dst_ref=dst,
            send_sem=ss,
            recv_sem=rs,
            device_id=dev,
            device_id_type=MESH,
        )

    def send(src, dst, ss, rs, dev):
        copy = desc(src, dst, ss, rs, dev)
        copy.start()
        sent.append(copy)

    def arrive(dst, ss, rs):
        desc(dst, dst, ss, rs, sib).wait_recv()

    def a_block(b, yy):
        return a_buf.at[b * 4 + mod4(yy)]

    def a_y_start(b):
        for t, d in enumerate((1, -1)):
            ref = a_block(b, y)
            send(ref, ref, ay_send.at[b, t], ay_recv.at[b, t], y_dev[d])

    def a_y_forward(b):
        for t, d in enumerate((1, -1)):
            ref = a_block(b, y - d)
            arrive(ref, ay_send.at[b, t], ay_recv.at[b, t])
            half = ref.at[t]
            send(half, half, ay_send.at[b, 2 + t], ay_recv.at[b, 2 + t], y_dev[d])

    def a_y_finish(b):
        for t in range(2):
            half = a_block(b, y + 2).at[t]
            arrive(half, ay_send.at[b, 2 + t], ay_recv.at[b, 2 + t])

    conditional = []

    def a_z_send(cond, b, dev_zl, ss):
        ref = a_block(b, y)
        copy = desc(ref, ref, ss, az_recv.at[b], (row, dev_zl * 4 + y))
        pl.when(cond)(copy.start)
        conditional.append((cond, copy))

    other = [
        jnp.where(zl == 0, 1, jnp.where(zl == 1, 0, jnp.where(zl == 2, 1, 2))),
        jnp.where(zl == 0, 2, jnp.where(zl == 1, 2, jnp.where(zl == 2, 3, 1))),
        jnp.where(zl == 0, 3, jnp.where(zl == 1, 3, 0)),
    ]

    def a_z_step(i):
        b = other[i]
        arrive(a_block(b, y), az_fwd.at[b], az_recv.at[b])
        from_left = b < zl
        dev_zl = jnp.where(from_left, zl + 1, zl - 1)
        a_z_send((dev_zl >= 0) & (dev_zl <= 3), b, mod4(dev_zl), az_fwd.at[b])
        a_y_start(b)

    offsets = (0, -1, 1, 2)

    def l_block(m, k, dx):
        return l_buf[m].at[row_of(x + dx, zh + offsets[k], c)]

    def l_sib_block(m, k, dx):
        return l_buf[m].at[row_of(x + dx, zh + offsets[k], 1 - c)]

    def l_relay(m, k, t):
        ref = l_block(m, k, offsets[t])
        send(ref, ref, lc_send.at[m, k, t], lc_recv.at[m, k, t], sib)

    def l_z_start(m):
        ref = l_block(m, 0, 0)
        for t, d in enumerate((1, -1)):
            send(ref, ref, lz_send.at[m, t], lz_recv.at[m, t], zh_dev[d])

    def l_z_forward(m):
        for t, d in enumerate((1, -1)):
            ref = l_block(m, 1 + t, 0)
            arrive(ref, lz_send.at[m, t], lz_recv.at[m, t])
            half = ref.at[t]
            send(half, half, lz_send.at[m, 2 + t], lz_recv.at[m, 2 + t], zh_dev[d])
            l_x_start(m, 1 + t)

    def l_z_finish(m):
        for t in range(2):
            half = l_block(m, 3, 0).at[t]
            arrive(half, lz_send.at[m, 2 + t], lz_recv.at[m, 2 + t])
        l_x_start(m, 3)

    def l_x_start(m, k):
        ref = l_block(m, k, 0)
        for t, d in enumerate((1, -1)):
            send(ref, ref, lx_send.at[m, k, t], lx_recv.at[m, k, t], x_dev[d])
        l_relay(m, k, 0)

    def l_x_forward(m, k):
        for t, d in enumerate((1, -1)):
            ref = l_block(m, k, -d)
            arrive(ref, lx_send.at[m, k, t], lx_recv.at[m, k, t])
            half = ref.at[t]
            send(half, half, lx_send.at[m, k, 2 + t], lx_recv.at[m, k, 2 + t], x_dev[d])
            l_relay(m, k, 1 + t)

    def l_x_finish(m, k):
        for t in range(2):
            half = l_block(m, k, 2).at[t]
            arrive(half, lx_send.at[m, k, 2 + t], lx_recv.at[m, k, 2 + t])
        l_relay(m, k, 3)

    def l_sib_finish(m):
        for k in range(4):
            for t in range(4):
                arrive(l_sib_block(m, k, offsets[t]), lc_send.at[m, k, t], lc_recv.at[m, k, t])

    block_row = row // 2

    def leaf_state(m):
        count = counts_ref[m]
        place, live = jnp.int32(0), jnp.int32(0)
        for q in range(SLOTS):
            hit = ((rows_ref[m, q] == block_row) & (count > q)).astype(jnp.int32)
            place += hit * q
            live += hit
        return count, place, live

    def compute(m):
        count, place, live = leaf_state(m)
        acc[...] = jnp.zeros_like(acc)

        def step(q, carry):
            active = (count > q).astype(jnp.int32).astype(jnp.float32)
            left = a_buf[rows_ref[m, q]].reshape(B, B)
            a_high, a_low = split(left)
            for part in range(2):
                right = l_buf[m][pl.ds(q * 4, 4), part].reshape(B, B) * active
                r_high, r_low = split(right)
                acc[part] += dot(a_high, r_high) + (dot(a_low, r_high) + dot(a_high, r_low))
            return carry

        lax.fori_loop(0, SLOTS, step, 0)
        keep = -(live.astype(jnp.float32))
        half = B // 2
        real = (acc[0, :half] - acc[1, half:]) * keep
        imag = (acc[1, :half] + acc[0, half:]) * keep
        sel_ref[0, :, pl.ds(m * B, B)] = real
        sel_ref[1, :, pl.ds(m * B, B)] = imag

    def diagonal(m):
        count, place, live = leaf_state(m)
        half = B // 2
        real = sel_ref[0, :, pl.ds(m * B, B)]
        imag = sel_ref[1, :, pl.ds(m * B, B)]
        low = l_buf[m][pl.ds(place * 4 + c * 2, 2)]
        low_real, low_imag = low[:, 0].reshape(half, B), low[:, 1].reshape(half, B)
        for part in range(2):
            if part == 0:
                left = jnp.concatenate([real, -imag], axis=0)
                right = jnp.concatenate([low_real, low_imag], axis=0)
            else:
                left = jnp.concatenate([real, imag], axis=0)
                right = jnp.concatenate([low_imag, low_real], axis=0)
            l_high, l_low = split(left)
            r_high, r_low = split(right)
            value = dot_t(l_high, r_high) + (dot_t(l_low, r_high) + dot_t(l_high, r_low))
            d_buf[m, :, :, part] = value.reshape(16, 2, 8, B)

    def rs0(m):
        send(d_buf.at[m, :, 1 - c], sib_buf.at[m], rs_send.at[m, 0], rs_recv.at[m, 0], sib)

    def rs1(m):
        arrive(sib_buf.at[m], rs_send.at[m, 0], rs_recv.at[m, 0])
        c_buf[m] = (d_buf[m, :, c] + sib_buf[m]).reshape(4, 4, 2, 8, B)
        for t, d in enumerate((1, -1)):
            send(
                c_buf.at[m, mod4(x + 2), :, t],
                x1_buf.at[m, t],
                rs_send.at[m, 1 + t],
                rs_recv.at[m, 1 + t],
                x_dev[d],
            )

    def rs2(m):
        for t, d in enumerate((1, -1)):
            arrive(x1_buf.at[m, t], rs_send.at[m, 1 + t], rs_recv.at[m, 1 + t])
            place = mod4(x + d)
            c_buf[m, place, :, t] = c_buf[m, place, :, t] + x1_buf[m, t]
            send(
                c_buf.at[m, place],
                x2_buf.at[m, t],
                rs_send.at[m, 3 + t],
                rs_recv.at[m, 3 + t],
                x_dev[d],
            )

    def rs3(m):
        for t in range(2):
            arrive(x2_buf.at[m, t], rs_send.at[m, 3 + t], rs_recv.at[m, 3 + t])
        e_buf[m] = c_buf[m, x] + (x2_buf[m, 0] + x2_buf[m, 1])
        for t, d in enumerate((1, -1)):
            send(
                e_buf.at[m, mod4(zh + 2), t],
                z1_buf.at[m, t],
                rs_send.at[m, 5 + t],
                rs_recv.at[m, 5 + t],
                zh_dev[d],
            )

    def rs4(m):
        for t, d in enumerate((1, -1)):
            arrive(z1_buf.at[m, t], rs_send.at[m, 5 + t], rs_recv.at[m, 5 + t])
            place = mod4(zh + d)
            e_buf[m, place, t] = e_buf[m, place, t] + z1_buf[m, t]
            send(
                e_buf.at[m, place],
                z2_buf.at[m, t],
                rs_send.at[m, 7 + t],
                rs_recv.at[m, 7 + t],
                zh_dev[d],
            )

    def rs5(m):
        for t in range(2):
            arrive(z2_buf.at[m, t], rs_send.at[m, 7 + t], rs_recv.at[m, 7 + t])
        total = e_buf[m, zh] + (z2_buf[m, 0] + z2_buf[m, 1])
        out_ref[:, :, pl.ds(m * B, B)] = diag_ref[:, :, pl.ds(m * B, B)] - total

    a_z_send(zl < 3, zl, mod4(zl + 1), az_own.at[0])
    a_z_send(zl > 0, zl, mod4(zl - 1), az_own.at[1])
    a_y_start(zl)
    l_z_start(0)
    l_x_start(0, 0)
    l_x_start(1, 0)
    a_z_step(0)
    a_y_forward(zl)
    l_x_forward(0, 0)
    l_x_forward(1, 0)
    l_x_finish(0, 0)
    l_x_finish(1, 0)
    a_z_step(1)
    l_z_forward(0)
    l_z_start(1)
    a_y_forward(other[0])
    a_y_finish(zl)
    l_x_forward(0, 1)
    l_x_forward(0, 2)
    a_z_step(2)
    a_y_forward(other[1])
    a_y_finish(other[0])
    l_z_finish(0)
    l_x_finish(0, 1)
    l_x_finish(0, 2)
    l_z_forward(1)
    a_y_forward(other[2])
    a_y_finish(other[1])
    l_x_forward(0, 3)
    l_x_forward(1, 1)
    l_x_forward(1, 2)
    a_y_finish(other[2])
    l_x_finish(0, 3)
    l_x_finish(1, 1)
    l_x_finish(1, 2)
    l_sib_finish(0)
    compute(0)
    diagonal(0)
    rs0(0)
    l_z_finish(1)
    l_x_forward(1, 3)
    rs1(0)
    l_x_finish(1, 3)
    l_sib_finish(1)
    compute(1)
    diagonal(1)
    rs0(1)
    rs2(0)
    rs1(1)
    rs3(0)
    rs2(1)
    rs4(0)
    rs3(1)
    rs5(0)
    rs4(1)
    rs5(1)
    for copy in sent:
        copy.wait_send()
    for cond, copy in conditional:
        pl.when(cond)(copy.wait_send)


def on_device(top_inverse, panel, leaf_rows, leaf_counts, diag_inverse):
    f32 = jnp.float32
    any_space = pl.BlockSpec(memory_space=pl.ANY)
    vmem = pl.BlockSpec(memory_space=pltpu.VMEM)
    smem = pl.BlockSpec(memory_space=pltpu.SMEM)
    dma = pltpu.SemaphoreType.DMA
    return pl.pallas_call(
        kernel,
        out_shape=(
            jax.ShapeDtypeStruct((2, B // 2, LEAVES * B), f32),
            jax.ShapeDtypeStruct((2, 8, LEAVES * B), f32),
        ),
        in_specs=[smem, smem, any_space, any_space, vmem],
        out_specs=(vmem, vmem),
        scratch_shapes=[
            pltpu.VMEM((16, 2, B // 2, B), f32),
            pltpu.VMEM((32, 2, 64, B), f32),
            pltpu.VMEM((32, 2, 64, B), f32),
            pltpu.VMEM((2, B, B), f32),
            pltpu.VMEM((LEAVES, 16, 2, 2, 8, B), f32),
            pltpu.VMEM((LEAVES, 16, 2, 8, B), f32),
            pltpu.VMEM((LEAVES, 4, 4, 2, 8, B), f32),
            pltpu.VMEM((LEAVES, 2, 4, 8, B), f32),
            pltpu.VMEM((LEAVES, 2, 4, 2, 8, B), f32),
            pltpu.VMEM((LEAVES, 4, 2, 8, B), f32),
            pltpu.VMEM((LEAVES, 2, 8, B), f32),
            pltpu.VMEM((LEAVES, 2, 2, 8, B), f32),
            dma((3,)),
            dma((2,)),
            dma((4,)),
            dma((4,)),
            dma((4, 4)),
            dma((4, 4)),
            dma((LEAVES, 4)),
            dma((LEAVES, 4)),
            dma((LEAVES, 4, 4)),
            dma((LEAVES, 4, 4)),
            dma((LEAVES, 4, 4)),
            dma((LEAVES, 4, 4)),
            dma((LEAVES, 9)),
            dma((LEAVES, 9)),
        ],
        compiler_params=pltpu.CompilerParams(collective_id=0, has_side_effects=True),
    )(leaf_rows, leaf_counts, top_inverse, panel, diag_inverse)


def solution(mesh):
    return jax.shard_map(
        on_device,
        mesh=mesh,
        in_specs=(
            P(None, "row", "col"),
            P(None, "row", "col"),
            P("col", None),
            P("col"),
            P(None, "row", "col"),
        ),
        out_specs=(P(None, "row", "col"), P(None, "row", "col")),
        check_vma=False,
    )
```

time: 627 us -> 120 us (0.19)
  waiting for transfers between devices: 500 us -> 0 us
  Pallas kernels: 0 us -> 116 us
  other arithmetic: 54.8 us -> 0 us
  local copies, waits for them, and re-layouts: 35.5 us -> 2.49 us
  matrix products: 22.6 us -> 0 us
  between operations: 14.1 us -> 0.65 us
    psum x1 -> x0, waiting for transfers between devices: 343 us -> none  [on_device(): total_sum = lax.psum(partial_diag, 'row')]
    all_gather x2 -> x0, waiting for transfers between devices: 156 us -> none  [the longest x1 103 us: on_device(): section = lax.all_gather(panel, 'row', axis=1, tiled=True)]
    pallas_call x0 -> x1, Pallas kernels: none -> 116 us  [on_device(): pl.pallas_call(kernel, out_shape=(jax.ShapeDtypeStruct((2, B // 2, LEAVES...]
    gather x3 -> x0, local copies, waits for them, and re-layouts: 26.4 us -> none  [the longest x2 25.6 us: on_device(): picked = jnp.take(top_strip, columns, axis=2)]
    dot_general x20 -> x0, matrix products: 22.6 us -> none  [product_highest(): jnp.dot(left, right, precision=lax.Precision.HIGHEST, preferred_element_t...]
    and x4 -> x0, other arithmetic: 21.3 us -> none  [the longest x2 11.2 us: on_device(): owned = slot_active & (slot_target_block == my_block)]
    select_n x2 -> x0, other arithmetic: 14.9 us -> none  [on_device(): picked = jnp.take(top_strip, columns, axis=2)]
    gather x2 -> x0, other arithmetic: 10.1 us -> none
  transfers between devices with their start and end apart: 3 -> 0, of which waited for: 3 -> 0; matrix products, arithmetic and copies ran while one was open for 13% -> 0% of each run, Pallas kernels for 0% -> 0%
where the time goes in v1:
time: 120 us; the launch traced here: 119 us
  Pallas kernels  116 us (97%)
  local copies, waits for them, and re-layouts  2.49 us (2%)
    pallas_call x1, Pallas kernels, on_device(): pl.pallas_call(kernel, out_shape=(jax.ShapeDtypeStruct((2, B // 2, LEAVES...  116 us
    unnamed x4, local copies, waits for them, and re-layouts  2.49 us

profile of v1, /device:TPU:1, one launch (start us, length us, event | category | flops | bytes accessed | tf_op | source)
XLA Modules:
  0.0 118.7 jit_solution(16421614834847586152)
XLA Ops:
  0.6 115.5 %shard_map.68 = (f32[2,128,512]{2,1,0:T(8,128)}, f32[2,8,512]{2,1,0:T(8,128)}) custom-call(s32[2,8]{1,0:T(2,128)} %rows_ref.1, s32[2]{0:T(128)} %counts_ref.1, f32[2,128,256]{2,1,0:T(8,128)} %top_ref.1, f32[2,64,512]{2,1,0:T(8,128)} %panel_ref.1, f32[2,8,512]{2,1,0:T(8,128)} %diag_ref.1), custom_call_target="tpu_custom_call" | custom-call | tf_op jit(solution)/shard_map/pallas_call | solution.py:401
  116.2 0.0 copy-start
  116.2 1.9 %copy.9 = f32[2,128,512]{2,1,0:T(8,128)} copy(f32[2,128,512]{2,1,0:T(8,128)} %get-tuple-element.4) | data formatting | bytes 1048576
  118.1 0.0 copy-done
  118.1 0.6 copy.10
Async XLA Ops:
  116.2 1.9 %copy-start = (f32[2,8,512]{2,1,0:T(8,128)S(1)}, f32[2,8,512]{2,1,0:T(8,128)}, u32[]{:S(2)}) copy-start(f32[2,8,512]{2,1,0:T(8,128)} %get-tuple-element.5) | copy-start | bytes 98308

commit v2 on v1

--- a/solution.py
+++ b/solution.py
@@ -9,7 +9,8 @@
 B = 256
 SLOTS = 8
 LEAVES = 2
-RING = 4
+CHUNKS = ((0, 0, 256), (1, 0, 128), (1, 128, 128))
+NC = len(CHUNKS)
 
 
 def split(value):
@@ -39,6 +40,7 @@
     a_buf,
     l_buf0,
     l_buf1,
+    a_hl,
     acc,
     d_buf,
     sib_buf,
@@ -135,6 +137,13 @@
             half = ref.at[t]
             send(half, half, ay_send.at[b, 2 + t], ay_recv.at[b, 2 + t], y_dev[d])
 
+    def a_y_forward1(b, t):
+        d = (1, -1)[t]
+        ref = a_block(b, y - d)
+        arrive(ref, ay_send.at[b, t], ay_recv.at[b, t])
+        half = ref.at[t]
+        send(half, half, ay_send.at[b, 2 + t], ay_recv.at[b, 2 + t], y_dev[d])
+
     def a_y_finish(b):
         for t in range(2):
             half = a_block(b, y + 2).at[t]
@@ -147,6 +156,12 @@
         copy = desc(ref, ref, ss, az_recv.at[b], (row, dev_zl * 4 + y))
         pl.when(cond)(copy.start)
         conditional.append((cond, copy))
+
+    def a_z_own(i):
+        if i == 0:
+            a_z_send(zl < 3, zl, mod4(zl + 1), az_own.at[0])
+        else:
+            a_z_send(zl > 0, zl, mod4(zl - 1), az_own.at[1])
 
     other = [
         jnp.where(zl == 0, 1, jnp.where(zl == 1, 0, jnp.where(zl == 2, 1, 2))),
@@ -165,10 +180,12 @@
     offsets = (0, -1, 1, 2)
 
     def l_block(m, k, dx):
-        return l_buf[m].at[row_of(x + dx, zh + offsets[k], c)]
+        leaf, off, width = CHUNKS[m]
+        return l_buf[leaf].at[row_of(x + dx, zh + offsets[k], c), :, :, pl.ds(off, width)]
 
     def l_sib_block(m, k, dx):
-        return l_buf[m].at[row_of(x + dx, zh + offsets[k], 1 - c)]
+        leaf, off, width = CHUNKS[m]
+        return l_buf[leaf].at[row_of(x + dx, zh + offsets[k], 1 - c), :, :, pl.ds(off, width)]
 
     def l_relay(m, k, t):
         ref = l_block(m, k, offsets[t])
@@ -178,6 +195,25 @@
         ref = l_block(m, 0, 0)
         for t, d in enumerate((1, -1)):
             send(ref, ref, lz_send.at[m, t], lz_recv.at[m, t], zh_dev[d])
+
+    def l_z_start1(m, t):
+        ref = l_block(m, 0, 0)
+        send(ref, ref, lz_send.at[m, t], lz_recv.at[m, t], zh_dev[(1, -1)[t]])
+
+    def l_z_forward1(m, t):
+        ref = l_block(m, 1 + t, 0)
+        arrive(ref, lz_send.at[m, t], lz_recv.at[m, t])
+        half = ref.at[t]
+        send(half, half, lz_send.at[m, 2 + t], lz_recv.at[m, 2 + t], zh_dev[(1, -1)[t]])
+        l_x_start(m, 1 + t)
+
+    def l_x_forward1(m, k, t):
+        d = (1, -1)[t]
+        ref = l_block(m, k, -d)
+        arrive(ref, lx_send.at[m, k, t], lx_recv.at[m, k, t])
+        half = ref.at[t]
+        send(half, half, lx_send.at[m, k, 2 + t], lx_recv.at[m, k, 2 + t], x_dev[d])
+        l_relay(m, k, 1 + t)
 
     def l_z_forward(m):
         for t, d in enumerate((1, -1)):
@@ -213,8 +249,13 @@
             arrive(half, lx_send.at[m, k, 2 + t], lx_recv.at[m, k, 2 + t])
         l_relay(m, k, 3)
 
-    def l_sib_finish(m):
-        for k in range(4):
+    def l_sib_group(m, group):
+        for k in (0, 1, 2) if group == 0 else (3,):
+            for t in range(4):
+                arrive(l_sib_block(m, k, offsets[t]), lc_send.at[m, k, t], lc_recv.at[m, k, t])
+
+    def l_sib_group(m, group):
+        for k in (0, 1, 2) if group == 0 else (3,):
             for t in range(4):
                 arrive(l_sib_block(m, k, offsets[t]), lc_send.at[m, k, t], lc_recv.at[m, k, t])
 
@@ -229,27 +270,40 @@
             live += hit
         return count, place, live
 
-    def compute(m):
+    def a_split(b):
+        def one(t, carry):
+            high, low = split(a_buf[b * 4 + t].reshape(B, B))
+            a_hl[b * 4 + t, :B] = high
+            a_hl[b * 4 + t, B:] = low
+            return carry
+
+        lax.fori_loop(0, 4, one, 0)
+
+    def compute(m, group):
         count, place, live = leaf_state(m)
-        acc[...] = jnp.zeros_like(acc)
-
-        def step(q, carry):
-            active = (count > q).astype(jnp.int32).astype(jnp.float32)
-            left = a_buf[rows_ref[m, q]].reshape(B, B)
-            a_high, a_low = split(left)
-            for part in range(2):
-                right = l_buf[m][pl.ds(q * 4, 4), part].reshape(B, B) * active
-                r_high, r_low = split(right)
-                acc[part] += dot(a_high, r_high) + (dot(a_low, r_high) + dot(a_high, r_low))
-            return carry
-
-        lax.fori_loop(0, SLOTS, step, 0)
-        keep = -(live.astype(jnp.float32))
-        half = B // 2
-        real = (acc[0, :half] - acc[1, half:]) * keep
-        imag = (acc[1, :half] + acc[0, half:]) * keep
-        sel_ref[0, :, pl.ds(m * B, B)] = real
-        sel_ref[1, :, pl.ds(m * B, B)] = imag
+        parity = zh // 2 if group == 0 else 1 - zh // 2
+        slots = [2 * i + parity for i in range(4)]
+        left = jnp.concatenate([a_hl[rows_ref[m, q]] for q in slots], axis=1)
+        for part in range(2):
+            rights = [
+                l_buf[m][pl.ds(q * 4, 4), part].reshape(B, B)
+                * (count > q).astype(jnp.int32).astype(jnp.float32)
+                for q in slots
+            ]
+            r_high, r_low = split(jnp.concatenate(rights, axis=0))
+            both = dot(left, r_high)
+            value = both[:B] + (both[B:] + dot(left[:B], r_low))
+            if group == 0:
+                acc[m, part] = value
+            else:
+                acc[m, part] += value
+        if group == 1:
+            keep = -(live.astype(jnp.float32))
+            half = B // 2
+            real = (acc[m, 0, :half] - acc[m, 1, half:]) * keep
+            imag = (acc[m, 1, :half] + acc[m, 0, half:]) * keep
+            sel_ref[0, :, pl.ds(m * B, B)] = real
+            sel_ref[1, :, pl.ds(m * B, B)] = imag
 
     def diagonal(m):
         count, place, live = leaf_state(m)
@@ -330,62 +384,106 @@
         total = e_buf[m, zh] + (z2_buf[m, 0] + z2_buf[m, 1])
         out_ref[:, :, pl.ds(m * B, B)] = diag_ref[:, :, pl.ds(m * B, B)] - total
 
-    a_z_send(zl < 3, zl, mod4(zl + 1), az_own.at[0])
-    a_z_send(zl > 0, zl, mod4(zl - 1), az_own.at[1])
+    l_x_start(1,0)
+    a_z_own(0)
+    l_z_start1(0,0)
+    l_z_start1(1,0)
+    l_x_start(2,0)
+    a_z_own(1)
+    l_x_start(0,0)
+    l_z_start1(1,1)
+    l_z_start1(0,1)
+    a_z_step(0)
     a_y_start(zl)
-    l_z_start(0)
-    l_x_start(0, 0)
-    l_x_start(1, 0)
-    a_z_step(0)
-    a_y_forward(zl)
-    l_x_forward(0, 0)
-    l_x_forward(1, 0)
-    l_x_finish(0, 0)
-    l_x_finish(1, 0)
     a_z_step(1)
-    l_z_forward(0)
-    l_z_start(1)
-    a_y_forward(other[0])
+    l_z_forward1(0,0)
+    l_z_forward1(1,0)
+    l_z_forward1(0,1)
+    l_x_forward1(0,2,1)
+    l_x_forward1(2,0,0)
+    l_z_start1(2,1)
+    l_x_forward1(0,0,1)
+    l_x_forward1(1,0,1)
+    a_y_forward1(other[0],0)
+    l_x_forward1(1,0,0)
+    a_y_forward1(other[1],1)
+    a_y_forward1(other[0],1)
+    l_x_forward1(2,0,1)
+    l_x_forward1(0,1,0)
+    a_y_forward1(zl,1)
+    l_x_forward1(0,2,0)
+    l_x_forward1(1,1,1)
+    l_z_start1(2,0)
+    l_x_forward1(0,0,0)
+    a_y_forward1(other[1],0)
+    l_z_forward1(1,1)
+    a_y_forward1(zl,0)
+    l_z_finish(0)
+    l_x_forward1(0,1,1)
+    a_y_finish(other[0])
+    l_x_finish(0,2)
+    a_z_step(2)
+    l_z_forward1(2,1)
+    l_z_finish(1)
+    l_x_forward1(1,2,1)
+    a_y_finish(other[1])
+    l_x_finish(0,1)
+    l_x_forward1(1,1,0)
+    l_z_forward1(2,0)
+    l_x_forward1(1,2,0)
+    l_x_finish(1,0)
+    l_x_finish(0,0)
+    l_z_finish(2)
+    l_x_forward1(0,3,1)
+    a_split(other[0])
+    l_x_forward1(0,3,0)
+    l_x_forward1(2,1,1)
+    a_y_forward1(other[2],0)
+    l_x_finish(1,2)
+    a_y_forward1(other[2],1)
+    l_x_forward1(2,2,1)
+    l_x_finish(2,0)
+    a_split(other[1])
     a_y_finish(zl)
-    l_x_forward(0, 1)
-    l_x_forward(0, 2)
-    a_z_step(2)
-    a_y_forward(other[1])
-    a_y_finish(other[0])
-    l_z_finish(0)
-    l_x_finish(0, 1)
-    l_x_finish(0, 2)
-    l_z_forward(1)
-    a_y_forward(other[2])
-    a_y_finish(other[1])
-    l_x_forward(0, 3)
-    l_x_forward(1, 1)
-    l_x_forward(1, 2)
+    l_sib_group(0,0)
+    l_x_forward1(2,1,0)
+    l_x_finish(1,1)
+    l_x_forward1(2,2,0)
+    l_sib_group(1,0)
+    l_x_finish(2,1)
+    l_x_finish(0,3)
+    l_x_finish(2,2)
+    l_x_forward1(1,3,0)
     a_y_finish(other[2])
-    l_x_finish(0, 3)
-    l_x_finish(1, 1)
-    l_x_finish(1, 2)
-    l_sib_finish(0)
-    compute(0)
+    l_x_forward1(2,3,1)
+    l_x_forward1(1,3,1)
+    a_split(other[2])
+    a_split(zl)
+    compute(0,0)
+    l_x_forward1(2,3,0)
+    l_sib_group(0,1)
+    l_sib_group(2,0)
+    compute(1,0)
+    compute(0,1)
+    l_x_finish(1,3)
+    l_x_finish(2,3)
     diagonal(0)
+    l_sib_group(1,1)
     rs0(0)
-    l_z_finish(1)
-    l_x_forward(1, 3)
-    rs1(0)
-    l_x_finish(1, 3)
-    l_sib_finish(1)
-    compute(1)
+    l_sib_group(2,1)
+    compute(1,1)
     diagonal(1)
     rs0(1)
+    rs1(0)
+    rs1(1)
     rs2(0)
-    rs1(1)
+    rs2(1)
     rs3(0)
-    rs2(1)
+    rs3(1)
     rs4(0)
-    rs3(1)
-    rs5(0)
     rs4(1)
     rs5(1)
+    rs5(0)
     for copy in sent:
         copy.wait_send()
     for cond, copy in conditional:
@@ -401,8 +499,8 @@
     return pl.pallas_call(
         kernel,
         out_shape=(
-            jax.ShapeDtypeStruct((2, B // 2, LEAVES * B), f32),
-            jax.ShapeDtypeStruct((2, 8, LEAVES * B), f32),
+            pltpu.VMEM((2, B // 2, LEAVES * B), f32),
+            pltpu.VMEM((2, 8, LEAVES * B), f32),
         ),
         in_specs=[smem, smem, any_space, any_space, vmem],
         out_specs=(vmem, vmem),
@@ -410,7 +508,8 @@
             pltpu.VMEM((16, 2, B // 2, B), f32),
             pltpu.VMEM((32, 2, 64, B), f32),
             pltpu.VMEM((32, 2, 64, B), f32),
-            pltpu.VMEM((2, B, B), f32),
+            pltpu.VMEM((16, 2 * B, B), jnp.bfloat16),
+            pltpu.VMEM((LEAVES, 2, B, B), f32),
             pltpu.VMEM((LEAVES, 16, 2, 2, 8, B), f32),
             pltpu.VMEM((LEAVES, 16, 2, 8, B), f32),
             pltpu.VMEM((LEAVES, 4, 4, 2, 8, B), f32),
@@ -425,12 +524,12 @@
             dma((4,)),
             dma((4, 4)),
             dma((4, 4)),
-            dma((LEAVES, 4)),
-            dma((LEAVES, 4)),
-            dma((LEAVES, 4, 4)),
-            dma((LEAVES, 4, 4)),
-            dma((LEAVES, 4, 4)),
-            dma((LEAVES, 4, 4)),
+            dma((NC, 4)),
+            dma((NC, 4)),
+            dma((NC, 4, 4)),
+            dma((NC, 4, 4)),
+            dma((NC, 4, 4)),
+            dma((NC, 4, 4)),
             dma((LEAVES, 9)),
             dma((LEAVES, 9)),
         ],

time: 120 us -> 108 us (0.900)
  Pallas kernels: 116 us -> 104 us
    pallas_call x1, Pallas kernels: 116 us -> 104 us  [on_device(): pl.pallas_call(kernel, out_shape=(pltpu.VMEM((2, B // 2, LEAVES * B), f32...]
    unnamed x4 -> x2, local copies, waits for them, and re-layouts: 2.49 us -> 1.41 us
where the time goes in v2:
time: 108 us; the launch traced here: 106 us
  Pallas kernels  104 us (96%)
  local copies, waits for them, and re-layouts  1.41 us (1%)
    pallas_call x1, Pallas kernels, on_device(): pl.pallas_call(kernel, out_shape=(pltpu.VMEM((2, B // 2, LEAVES * B), f32...  104 us

profile of v2, /device:TPU:1, one launch (start us, length us, event | category | flops | bytes accessed | tf_op | source)
XLA Modules:
  0.0 106.3 jit_solution(6713978299441221268)
XLA Ops:
  0.6 104.3 %shard_map.68 = (f32[2,128,512]{2,1,0:T(8,128)S(1)}, f32[2,8,512]{2,1,0:T(8,128)S(1)}) custom-call(s32[2,8]{1,0:T(2,128)} %rows_ref.1, s32[2]{0:T(128)} %counts_ref.1, f32[2,128,256]{2,1,0:T(8,128)} %top_ref.1, f32[2,64,512]{2,1,0:T(8,128)} %panel_ref.1, f32[2,8,512]{2,1,0:T(8,128)} %diag_ref.1), custom_call_target="tpu_custom_call" | custom-call | tf_op jit(solution)/shard_map/pallas_call | solution.py:499
  104.9 0.8 copy.9
  105.7 0.6 copy.10

commit v3 on v2

--- a/solution.py
+++ b/solution.py
@@ -9,7 +9,7 @@
 B = 256
 SLOTS = 8
 LEAVES = 2
-CHUNKS = ((0, 0, 256), (1, 0, 128), (1, 128, 128))
+CHUNKS = ((0, 0, 256), (1, 0, 256))
 NC = len(CHUNKS)
 
 
@@ -384,93 +384,73 @@
         total = e_buf[m, zh] + (z2_buf[m, 0] + z2_buf[m, 1])
         out_ref[:, :, pl.ds(m * B, B)] = diag_ref[:, :, pl.ds(m * B, B)] - total
 
+    a_z_own(0)
     l_x_start(1,0)
-    a_z_own(0)
     l_z_start1(0,0)
-    l_z_start1(1,0)
-    l_x_start(2,0)
+    l_z_start1(0,1)
+    l_x_start(0,0)
+    l_x_forward1(0,0,1)
     a_z_own(1)
-    l_x_start(0,0)
-    l_z_start1(1,1)
-    l_z_start1(0,1)
+    a_y_start(zl)
     a_z_step(0)
-    a_y_start(zl)
+    l_z_forward1(0,1)
     a_z_step(1)
     l_z_forward1(0,0)
-    l_z_forward1(1,0)
-    l_z_forward1(0,1)
+    l_x_forward1(0,2,0)
+    a_y_forward1(other[1],0)
+    a_y_forward1(other[0],0)
+    a_y_forward1(other[1],1)
+    a_y_forward1(zl,0)
+    l_x_forward1(0,1,0)
+    l_x_forward1(0,0,0)
+    l_z_start1(1,1)
+    l_z_start1(1,0)
+    a_y_forward1(zl,1)
     l_x_forward1(0,2,1)
-    l_x_forward1(2,0,0)
-    l_z_start1(2,1)
-    l_x_forward1(0,0,1)
-    l_x_forward1(1,0,1)
-    a_y_forward1(other[0],0)
-    l_x_forward1(1,0,0)
-    a_y_forward1(other[1],1)
-    a_y_forward1(other[0],1)
-    l_x_forward1(2,0,1)
-    l_x_forward1(0,1,0)
-    a_y_forward1(zl,1)
-    l_x_forward1(0,2,0)
-    l_x_forward1(1,1,1)
-    l_z_start1(2,0)
-    l_x_forward1(0,0,0)
-    a_y_forward1(other[1],0)
-    l_z_forward1(1,1)
-    a_y_forward1(zl,0)
+    l_x_finish(0,2)
     l_z_finish(0)
     l_x_forward1(0,1,1)
+    a_y_finish(other[1])
+    a_y_forward1(other[0],1)
+    a_z_step(2)
+    l_z_forward1(1,1)
+    l_x_forward1(1,0,1)
+    l_z_forward1(1,0)
+    l_x_finish(0,0)
+    a_y_finish(zl)
+    l_x_forward1(0,3,1)
+    l_x_forward1(1,0,0)
+    l_x_forward1(0,3,0)
+    a_y_forward1(other[2],0)
     a_y_finish(other[0])
-    l_x_finish(0,2)
-    a_z_step(2)
-    l_z_forward1(2,1)
-    l_z_finish(1)
+    a_y_forward1(other[2],1)
     l_x_forward1(1,2,1)
-    a_y_finish(other[1])
-    l_x_finish(0,1)
-    l_x_forward1(1,1,0)
-    l_z_forward1(2,0)
     l_x_forward1(1,2,0)
     l_x_finish(1,0)
-    l_x_finish(0,0)
-    l_z_finish(2)
-    l_x_forward1(0,3,1)
+    a_split(other[1])
+    l_x_finish(0,3)
+    l_z_finish(1)
+    a_split(zl)
+    l_x_finish(0,1)
     a_split(other[0])
-    l_x_forward1(0,3,0)
-    l_x_forward1(2,1,1)
-    a_y_forward1(other[2],0)
+    l_x_forward1(1,1,1)
+    a_y_finish(other[2])
+    l_sib_group(0,1)
+    l_sib_group(0,0)
+    l_x_forward1(1,1,0)
     l_x_finish(1,2)
-    a_y_forward1(other[2],1)
-    l_x_forward1(2,2,1)
-    l_x_finish(2,0)
-    a_split(other[1])
-    a_y_finish(zl)
-    l_sib_group(0,0)
-    l_x_forward1(2,1,0)
+    a_split(other[2])
+    compute(0,0)
+    l_x_forward1(1,3,0)
+    l_x_forward1(1,3,1)
+    compute(0,1)
     l_x_finish(1,1)
-    l_x_forward1(2,2,0)
+    diagonal(0)
+    l_x_finish(1,3)
+    rs0(0)
     l_sib_group(1,0)
-    l_x_finish(2,1)
-    l_x_finish(0,3)
-    l_x_finish(2,2)
-    l_x_forward1(1,3,0)
-    a_y_finish(other[2])
-    l_x_forward1(2,3,1)
-    l_x_forward1(1,3,1)
-    a_split(other[2])
-    a_split(zl)
-    compute(0,0)
-    l_x_forward1(2,3,0)
-    l_sib_group(0,1)
-    l_sib_group(2,0)
     compute(1,0)
-    compute(0,1)
-    l_x_finish(1,3)
-    l_x_finish(2,3)
-    diagonal(0)
     l_sib_group(1,1)
-    rs0(0)
-    l_sib_group(2,1)
     compute(1,1)
     diagonal(1)
     rs0(1)

time: 108 us -> 107 us (level); the launches traced: 106 us -> 107 us
  no operation moved by 1% of the time
where the time goes in v3:
time: 107 us
  Pallas kernels  104 us (97%)
  local copies, waits for them, and re-layouts  1.41 us (1%)
    pallas_call x1, Pallas kernels, on_device(): pl.pallas_call(kernel, out_shape=(pltpu.VMEM((2, B // 2, LEAVES * B), f32...  104 us

profile of v3, /device:TPU:1, one launch (start us, length us, event | category | flops | bytes accessed | tf_op | source)
XLA Modules:
  0.0 106.5 jit_solution(6264096255480595869)
XLA Ops:
  0.6 104.5 %shard_map.68 = (f32[2,128,512]{2,1,0:T(8,128)S(1)}, f32[2,8,512]{2,1,0:T(8,128)S(1)}) custom-call(s32[2,8]{1,0:T(2,128)} %rows_ref.1, s32[2]{0:T(128)} %counts_ref.1, f32[2,128,256]{2,1,0:T(8,128)} %top_ref.1, f32[2,64,512]{2,1,0:T(8,128)} %panel_ref.1, f32[2,8,512]{2,1,0:T(8,128)} %diag_ref.1), custom_call_target="tpu_custom_call" | custom-call | tf_op jit(solution)/shard_map/pallas_call | solution.py:479
  105.1 0.8 copy.9
  105.9 0.6 copy.10
